TPU v7x, 32 devices: a whole 2x2x4 slice. The times are simulated.
32 devices in a mesh: weight: 2 (over x), ctx: 4 (over z), tensor: 4 (over y, core).
Axes of the slice: x: 2, y: 2, z: 4, core: 2. Of those that a mesh axis runs over, the one named last changes fastest.
Arguments:
- inputs: bfloat16 [2, 1024, 1024], P('weight', 'ctx'), may hold values from -40 to 40
- w_qkv: bfloat16 [1024, 3, 1024], P('weight', None, 'tensor'), may hold values from -4 to 4
- w_out: bfloat16 [1024, 1024], P('weight', 'tensor'), may hold values from -2 to 2
- w_up: bfloat16 [1024, 4096], P('weight', 'tensor'), may hold values from -0.1875 to 0.1875
- w_down: bfloat16 [1024, 4096], P('weight', 'tensor'), may hold values from -0.09375 to 0.09375
- head_bias: float32 [2, 1024], P(None, 'tensor'), may hold values from -3 to 3
- up_bias: float32 [4096], P('tensor'), may hold values from -3 to 3
- out_biases: float32 [2, 1024], replicated, may hold values from -3 to 3
- norm_gains: float32 [2, 1024], replicated, may hold values from 0.1 to 1.9
- norm_shifts: float32 [2, 1024], replicated, may hold values from -3 to 3
- cotangent: bfloat16 [2, 1024, 1024], P('weight', 'ctx'), may hold values from -6 to 6
Outputs:
- layer_out: bfloat16 [2, 1024, 1024], P('weight', 'ctx')
- grad_input: bfloat16 [2, 1024, 1024], P('weight', 'ctx')
- grad_w_qkv: float32 [1024, 3, 1024], P(('weight', 'ctx'), None, 'tensor')
- grad_w_out: float32 [1024, 1024], P(('weight', 'ctx'), 'tensor')
- grad_w_up: float32 [1024, 4096], P(('weight', 'ctx'), 'tensor')
- grad_w_down: float32 [1024, 4096], P(('weight', 'ctx'), 'tensor')
- grad_head_bias: float32 [2, 1024], P(None, 'tensor')
- grad_up_bias: float32 [4096], P('tensor')
- grad_out_biases: float32 [2, 1024], replicated
- grad_norm_gains: float32 [2, 1024], replicated
- grad_norm_shifts: float32 [2, 1024], replicated
All inputs are finite; a program needn't handle non-finite values.
Results may differ from a plain program's by a relative error of at most 0.038.
Values may be sent and summed in bfloat16 or wider, within the bound.
No kernel may reach another device: no remote copies, remote signals or barrier semaphores. Data moves between devices by JAX's collectives and lax.ppermute only.
A program may use at most 128 MiB of HBM per device.

v0:
```python
import math
import jax
import jax.numpy as jnp
from jax import lax
from jax.sharding import PartitionSpec as P

HD = 64
norm_epsilon = 1e-05
inv_root_two = 1.0 / math.sqrt(2.0)
inv_root_tau = 1.0 / math.sqrt(2.0 * math.pi)


def layer_stats(hidden):
    mean_row = jnp.mean(hidden, axis=-1, keepdims=True)
    centred = hidden - mean_row
    inverse_spread = lax.rsqrt(jnp.mean(centred * centred, axis=-1, keepdims=True) + norm_epsilon)
    return (centred * inverse_spread, inverse_spread)


def layer_back(grad_norm, normed, inverse_spread):
    return inverse_spread * (
        grad_norm
        - jnp.mean(grad_norm, axis=-1, keepdims=True)
        - normed * jnp.mean(grad_norm * normed, axis=-1, keepdims=True)
    )


def gelu_value(pre_act):
    return 0.5 * pre_act * (1.0 + lax.erf(pre_act * inv_root_two))


def gelu_slope(pre_act):
    return (
        0.5 * (1.0 + lax.erf(pre_act * inv_root_two))
        + pre_act * jnp.exp(-0.5 * pre_act * pre_act) * inv_root_tau
    )


def heads_view(source):
    return source.reshape(source.shape[0], source.shape[1], -1, HD)


def settle(partial_value, row_work):
    return row_work(lax.psum(partial_value.astype(jnp.bfloat16), "tensor").astype(jnp.float32), 0)


def gather_keys(keys_flat, values_flat):
    return (
        lax.all_gather(keys_flat, "ctx", axis=1, tiled=True),
        lax.all_gather(values_flat, "ctx", axis=1, tiled=True),
    )


def key_blocks(state_now, query_heads, key_heads, value_heads, scale_factor):
    key_rows = key_heads.shape[1]
    block_size = math.gcd(512, key_rows)
    block_count = key_rows // block_size

    def one_block(state_in, block_index):
        acc_now, top_now, total_now = state_in
        key_part = lax.dynamic_slice_in_dim(key_heads, block_index * block_size, block_size, 1)
        value_part = lax.dynamic_slice_in_dim(value_heads, block_index * block_size, block_size, 1)
        scores = (
            jnp.einsum("bqhe,bkhe->bqhk", query_heads, key_part, preferred_element_type=jnp.float32)
            * scale_factor
        )
        top_next = jnp.maximum(top_now, jnp.max(scores, axis=-1))
        rescale = jnp.exp(top_now - top_next)
        weights = jnp.exp(scores - top_next[..., None])
        total_next = total_now * rescale + jnp.sum(weights, axis=-1)
        acc_next = acc_now * rescale[..., None] + jnp.einsum(
            "bqhk,bkhe->bqhe",
            weights.astype(jnp.bfloat16),
            value_part,
            preferred_element_type=jnp.float32,
        )
        return ((acc_next, top_next, total_next), None)

    state_out, ignored = lax.scan(one_block, state_now, jnp.arange(block_count))
    return state_out


def local(
    inputs,
    w_qkv,
    w_out,
    w_up,
    w_down,
    head_bias,
    up_bias,
    out_biases,
    norm_gains,
    norm_shifts,
    cotangent,
):
    batch, tok_rows = (inputs.shape[0], inputs.shape[1])
    head_cols = w_qkv.shape[2]
    heads_here = head_cols // HD
    scale_factor = HD ** (-0.5)
    qkv_full, out_full, up_full, down_full = (
        lax.all_gather(w_qkv, "weight", axis=0, tiled=True),
        lax.all_gather(w_out, "weight", axis=0, tiled=True),
        lax.all_gather(w_up, "weight", axis=0, tiled=True),
        lax.all_gather(w_down, "weight", axis=0, tiled=True),
    )
    projected = jnp.einsum("btd,dcf->btcf", inputs, qkv_full, preferred_element_type=jnp.float32)
    queries = (projected[:, :, 0] + head_bias[0]).astype(jnp.bfloat16)
    keys_flat = projected[:, :, 1].astype(jnp.bfloat16)
    values_flat = (projected[:, :, 2] + head_bias[1]).astype(jnp.bfloat16)
    query_heads = heads_view(queries)
    init_state = (
        jnp.zeros((batch, tok_rows, heads_here, HD), jnp.float32),
        jnp.full((batch, tok_rows, heads_here), -1e30, jnp.float32),
        jnp.zeros((batch, tok_rows, heads_here), jnp.float32),
    )
    state_end = key_blocks(
        init_state,
        query_heads,
        heads_view(lax.all_gather(keys_flat, "ctx", axis=1, tiled=True)),
        heads_view(lax.all_gather(values_flat, "ctx", axis=1, tiled=True)),
        scale_factor,
    )
    acc_sum, top_row, total_row = state_end
    log_sum = top_row + jnp.log(total_row)
    attended = (
        (acc_sum / total_row[..., None]).reshape(batch, tok_rows, head_cols).astype(jnp.bfloat16)
    )
    out_part = jnp.einsum("btf,of->bto", attended, out_full, preferred_element_type=jnp.float32)
    inputs_wide = inputs.astype(jnp.float32)

    def first_rows(summed, row_start):
        hidden = inputs_wide + summed + out_biases[0]
        return layer_stats(hidden)

    normed_one, inverse_one = settle(out_part, first_rows)
    mixed_one = normed_one * norm_gains[0] + norm_shifts[0]
    mixed_bf = mixed_one.astype(jnp.bfloat16)
    pre_act = (
        jnp.einsum("btd,df->btf", mixed_bf, up_full, preferred_element_type=jnp.float32) + up_bias
    )
    gelu_bf = gelu_value(pre_act).astype(jnp.bfloat16)
    down_part = jnp.einsum("btf,of->bto", gelu_bf, down_full, preferred_element_type=jnp.float32)

    def second_rows(summed, row_start):
        hidden = mixed_one + summed + out_biases[1]
        return layer_stats(hidden)

    normed_two, inverse_two = settle(down_part, second_rows)
    layer_out = (normed_two * norm_gains[1] + norm_shifts[1]).astype(jnp.bfloat16)
    grad_out = cotangent.astype(jnp.float32)
    grad_hidden_two = layer_back(grad_out * norm_gains[1], normed_two, inverse_two)
    gain_two = jnp.sum(grad_out * normed_two, axis=(0, 1))
    shift_two = jnp.sum(grad_out, axis=(0, 1))
    bias_down = jnp.sum(grad_hidden_two, axis=(0, 1))
    grad_two_bf = grad_hidden_two.astype(jnp.bfloat16)
    grad_down_w = jnp.einsum(
        "bto,btf->of", grad_two_bf, gelu_bf, preferred_element_type=jnp.float32
    )
    grad_pre = jnp.einsum(
        "bto,of->btf", grad_two_bf, down_full, preferred_element_type=jnp.float32
    ) * gelu_slope(pre_act)
    grad_up_b = jnp.sum(grad_pre, axis=(0, 1))
    grad_pre_bf = grad_pre.astype(jnp.bfloat16)
    grad_up_w = jnp.einsum("btd,btf->df", mixed_bf, grad_pre_bf, preferred_element_type=jnp.float32)
    mixed_part = jnp.einsum("btf,df->btd", grad_pre_bf, up_full, preferred_element_type=jnp.float32)

    def third_rows(summed, row_start):
        grad_mixed = grad_hidden_two + summed
        grad_hidden = layer_back(grad_mixed * norm_gains[0], normed_one, inverse_one)
        return (grad_hidden, grad_mixed)

    grad_hidden_one, grad_mixed_one = settle(mixed_part, third_rows)
    gain_one = jnp.sum(grad_mixed_one * normed_one, axis=(0, 1))
    shift_one = jnp.sum(grad_mixed_one, axis=(0, 1))
    bias_out = jnp.sum(grad_hidden_one, axis=(0, 1))
    grad_one_bf = grad_hidden_one.astype(jnp.bfloat16)
    grad_out_w = jnp.einsum(
        "bto,btf->of", grad_one_bf, attended, preferred_element_type=jnp.float32
    )
    grad_attended = jnp.einsum(
        "bto,of->btf", grad_one_bf, out_full, preferred_element_type=jnp.float32
    ).astype(jnp.bfloat16)
    grad_attended_heads = heads_view(grad_attended)
    row_delta = jnp.sum(
        grad_attended_heads.astype(jnp.float32) * heads_view(attended).astype(jnp.float32), axis=-1
    )
    keys_all, values_all = gather_keys(keys_flat, values_flat)
    key_heads = heads_view(keys_all)
    value_heads = heads_view(values_all)
    key_rows = key_heads.shape[1]
    block_size = math.gcd(512, key_rows)
    block_count = key_rows // block_size

    def back_block(state_in, block_index):
        grad_query, grad_keys, grad_values = state_in
        offset = block_index * block_size
        key_part = lax.dynamic_slice_in_dim(key_heads, offset, block_size, 1)
        value_part = lax.dynamic_slice_in_dim(value_heads, offset, block_size, 1)
        scores = (
            jnp.einsum("bqhe,bkhe->bqhk", query_heads, key_part, preferred_element_type=jnp.float32)
            * scale_factor
        )
        weights = jnp.exp(scores - log_sum[..., None])
        values_part = jnp.einsum(
            "bqhk,bqhe->bkhe",
            weights.astype(jnp.bfloat16),
            grad_attended_heads,
            preferred_element_type=jnp.float32,
        )
        grad_weights = jnp.einsum(
            "bqhe,bkhe->bqhk", grad_attended_heads, value_part, preferred_element_type=jnp.float32
        )
        grad_scores = (weights * (grad_weights - row_delta[..., None]) * scale_factor).astype(
            jnp.bfloat16
        )
        grad_query = grad_query + jnp.einsum(
            "bqhk,bkhe->bqhe", grad_scores, key_part, preferred_element_type=jnp.float32
        )
        keys_part = jnp.einsum(
            "bqhk,bqhe->bkhe", grad_scores, query_heads, preferred_element_type=jnp.float32
        )
        grad_keys = lax.dynamic_update_slice_in_dim(grad_keys, keys_part, offset, 1)
        grad_values = lax.dynamic_update_slice_in_dim(grad_values, values_part, offset, 1)
        return ((grad_query, grad_keys, grad_values), None)

    zeros_keys = jnp.zeros((batch, key_rows, heads_here, HD), jnp.float32)
    back_init = (jnp.zeros((batch, tok_rows, heads_here, HD), jnp.float32), zeros_keys, zeros_keys)
    back_end, ignored = lax.scan(back_block, back_init, jnp.arange(block_count))
    grad_query_all, grad_keys_all, grad_values_all = back_end
    grad_keys_mine, grad_values_mine = (
        lax.psum_scatter(
            grad_keys_all.reshape(batch, key_rows, head_cols).astype(jnp.bfloat16),
            "ctx",
            scatter_dimension=1,
            tiled=True,
        ).astype(jnp.float32),
        lax.psum_scatter(
            grad_values_all.reshape(batch, key_rows, head_cols).astype(jnp.bfloat16),
            "ctx",
            scatter_dimension=1,
            tiled=True,
        ).astype(jnp.float32),
    )
    grad_query_flat = grad_query_all.reshape(batch, tok_rows, head_cols)
    grad_heads_bias = jnp.stack(
        [jnp.sum(grad_query_flat, axis=(0, 1)), jnp.sum(grad_values_mine, axis=(0, 1))]
    )
    grad_qkv_bf = jnp.stack([grad_query_flat, grad_keys_mine, grad_values_mine], axis=2).astype(
        jnp.bfloat16
    )
    grad_qkv_w = jnp.einsum(
        "btd,btcf->dcf", inputs, grad_qkv_bf, preferred_element_type=jnp.float32
    )
    input_part = jnp.einsum(
        "btcf,dcf->btd", grad_qkv_bf, qkv_full, preferred_element_type=jnp.float32
    )

    def fourth_rows(summed, row_start):
        return (grad_hidden_one + summed,)

    settled = settle(input_part, fourth_rows)
    grad_input = settled[0].astype(jnp.bfloat16)
    owned_grads = (
        lax.psum_scatter(
            grad_qkv_w.astype(jnp.bfloat16), ("weight", "ctx"), scatter_dimension=0, tiled=True
        ).astype(jnp.float32),
        lax.psum_scatter(
            grad_out_w.astype(jnp.bfloat16), ("weight", "ctx"), scatter_dimension=0, tiled=True
        ).astype(jnp.float32),
        lax.psum_scatter(
            grad_up_w.astype(jnp.bfloat16), ("weight", "ctx"), scatter_dimension=0, tiled=True
        ).astype(jnp.float32),
        lax.psum_scatter(
            grad_down_w.astype(jnp.bfloat16), ("weight", "ctx"), scatter_dimension=0, tiled=True
        ).astype(jnp.float32),
    )
    vector_sums = lax.psum(
        (
            grad_heads_bias,
            grad_up_b,
            jnp.stack([bias_out, bias_down]),
            jnp.stack([gain_one, gain_two]),
            jnp.stack([shift_one, shift_two]),
        ),
        ("weight", "ctx"),
    )
    return (
        layer_out,
        grad_input,
        owned_grads[0],
        owned_grads[1],
        owned_grads[2],
        owned_grads[3],
        vector_sums[0],
        vector_sums[1],
        vector_sums[2],
        vector_sums[3],
        vector_sums[4],
    )


def solution(mesh):
    return jax.shard_map(
        local,
        mesh=mesh,
        in_specs=(
            P("weight", "ctx", None),
            P("weight", None, "tensor"),
            P("weight", "tensor"),
            P("weight", "tensor"),
            P("weight", "tensor"),
            P(None, "tensor"),
            P("tensor"),
            P(),
            P(),
            P(),
            P("weight", "ctx", None),
        ),
        out_specs=(
            P("weight", "ctx", None),
            P("weight", "ctx", None),
            P(("weight", "ctx"), None, "tensor"),
            P(("weight", "ctx"), "tensor"),
            P(("weight", "ctx"), "tensor"),
            P(("weight", "ctx"), "tensor"),
            P(None, "tensor"),
            P("tensor"),
            P(),
            P(),
            P(),
        ),
        check_vma=False,
    )
```

profile of v0, /device:TPU:0, one launch (start us, length us, event | category | flops | bytes accessed | tf_op | source)
XLA Modules:
  0.0 652.9 jit_solution(9684503517704552660)
XLA Ops:
  7.3 2.4 copy.48
  9.8 10.0 %all_gather.23 = bf16[1024,256]{1,0:T(8,128)(2,1)} all-gather(bf16[512,256]{1,0:T(8,128)(2,1)S(1)} %copy-done.25), channel_id=1, replica_groups=mesh['weight'=2,'ctx'=4,'tensor'=4] {'weight'}, dimensions={0}, use_global_device_ids=true | all-gather | bytes 786432 | tf_op jit(solution)/shard_map/all_gather | solution.py:102
  19.8 19.8 %all-gather.5.cloned.1.call-done = bf16[1024,3,256]{0,2,1:T(8,128)(2,1)} async-done(((bf16[512,3,256]{0,2,1:T(8,128)(2,1)}), bf16[1024,3,256]{0,2,1:T(8,128)(2,1)}) %all-gather.5.cloned.1.call-update) | async-done | bytes 1572880 | tf_op jit(solution)/shard_map/all_gather | solution.py:101
  39.7 2.0 convolution_bitcast_fusion.5
  41.8 15.5 %all-gather = bf16[1,1024,1,256]{1,3,2,0:T(8,128)(2,1)S(1)} all-gather(bf16[1,256,1,256]{1,3,2,0:T(8,128)(2,1)S(1)} %slice.57), channel_id=2, replica_groups=mesh['weight'=2,'ctx'=4,'tensor'=4] {'ctx'}, dimensions={1}, use_global_device_ids=true | all-gather | bytes 655360 | tf_op jit(solution)/shard_map/all_gather | solution.py:119
  57.3 16.8 %all_gather.22 = bf16[1,1024,256]{1,2,0:T(8,128)(2,1)} all-gather(bf16[1,256,256]{1,2,0:T(8,128)(2,1)S(1)} %fusion.72), channel_id=1, replica_groups=mesh['weight'=2,'ctx'=4,'tensor'=4] {'ctx'}, dimensions={1}, use_global_device_ids=true | all-gather | bytes 655360 | tf_op jit(solution)/shard_map/all_gather | solution.py:120
  74.3 7.3 %while.30 = (s32[]{:T(128)}, f32[1,256,4,64]{1,3,2,0:T(8,128)S(1)}, f32[1,256,4]{1,2,0:T(4,128)S(1)}, f32[1,256,4]{1,2,0:T(4,128)S(1)}, s32[2]{0:T(128)S(1)}, /*...) while((s32[]{:T(128)}, f32[1,256,4,64]{1,3,2,0:T(8,128)S(1)}, ...), condition=%wide.region_3.4_spmd.clone, body=%wide.region_0.3_spmd.clone.sunk | while | flops 138614784 | bytes 7536843 | solution.py:79
  74.3 0.6 dynamic_slice.56
  76.1 1.5 fusion.129
  79.7 1.5 fusion.129
  81.7 0.6 copy-done.21
  82.3 2.2 fusion.53
  84.6 0.7 all-gather.7.cloned.1.call-update
  86.0 32.2 %all-reduce.6.cloned.1.call-done = bf16[1,256,1024]{2,1,0:T(8,128)(2,1)} async-done(((bf16[1,256,1024]{2,1,0:T(8,128)(2,1)}), bf16[1,256,1024]{2,1,0:T(8,128)(2,1)}) %all-reduce.6.cloned.1.call-update) | async-done | bytes 524304 | tf_op jit(solution)/shard_map/psum | solution.py:44
  118.3 1.4 fusion.63
  119.6 1.4 multiply_reduce_fusion.3
  121.0 32.0 %all-gather.7.cloned.1.call-done = bf16[1024,1024]{1,0:T(8,128)(2,1)} async-done(((bf16[512,1024]{1,0:T(8,128)(2,1)}), bf16[1024,1024]{1,0:T(8,128)(2,1)}) %all-gather.7.cloned.1.call-update) | async-done | bytes 2097168 | tf_op jit(solution)/shard_map/all_gather | solution.py:103
  153.0 2.4 convolution_add_fusion
  155.5 32.1 %all-gather.9.cloned.1.call-done = bf16[1024,1024]{1,0:T(8,128)(2,1)} async-done(((bf16[512,1024]{1,0:T(8,128)(2,1)}), bf16[1024,1024]{1,0:T(8,128)(2,1)}) %all-gather.9.cloned.1.call-update) | async-done | bytes 2097168 | tf_op jit(solution)/shard_map/all_gather | solution.py:104
  187.6 3.1 fusion.51
  190.8 33.5 %all-reduce.8.cloned.1.call-done = bf16[1,256,1024]{2,1,0:T(8,128)(2,1)} async-done(((bf16[1,256,1024]{2,1,0:T(8,128)(2,1)}), bf16[1,256,1024]{2,1,0:T(8,128)(2,1)}) %all-reduce.8.cloned.1.call-update) | async-done | bytes 524304 | tf_op jit(solution)/shard_map/psum | solution.py:44
  224.3 1.7 fusion.85
  226.8 1.2 fusion.55
  228.2 1.0 fusion.91
  229.2 0.8 copy-done.31
  230.0 1.6 fusion.52
  231.9 33.4 %all-reduce.10.cloned.1.call-done = bf16[1,256,1024]{2,1,0:T(8,128)(2,1)} async-done(((bf16[1,256,1024]{2,1,0:T(8,128)(2,1)}), bf16[1,256,1024]{2,1,0:T(8,128)(2,1)}) %all-reduce.10.cloned.1.call-update) | async-done | bytes 524304 | tf_op jit(solution)/shard_map/psum | solution.py:44
  265.3 1.9 multiply_reduce_fusion
  267.8 1.0 copy-done.5
  269.2 0.9 broadcast_in_dim.10
  270.1 0.9 broadcast_in_dim.10.clone
  270.9 15.2 %while.31 = (s32[]{:T(128)}, f32[1,256,4,64]{1,3,2,0:T(8,128)}, bf16[1,1024,4,64]{1,3,2,0:T(8,128)(2,1)}, bf16[1,1024,4,64]{1,3,2,0:T(8,128)(2,1)}, s32[2]{0:T(1...) while((s32[]{:T(128)}, f32[1,256,4,64]{1,3,2,0:T(8,128)}, ...), condition=%wide.region_17.18_spmd.clone, body=%wide.region_16.17_spmd.clone.sunk | while | flops 340393984 | bytes 22819192 | solution.py:228
  270.9 0.7 dynamic_slice.60
  273.3 0.7 fusion.142
  274.1 2.0 fusion.143
  276.1 1.1 fusion.144
  277.7 0.8 copy-done.20
  278.5 0.7 dynamic_slice.60
  280.9 0.7 fusion.142
  281.6 2.1 fusion.143
  283.7 1.1 fusion.144
  285.4 0.8 copy-done.20
  286.2 2.1 copy.50
  288.4 2.0 copy.49
  290.5 1.2 convolution_convert_fusion.3
  292.0 18.3 %reduce-scatter.11.cloned.1.call-done = bf16[1,256,256]{2,1,0:T(8,128)(2,1)} async-done(((bf16[1,1024,256]{2,1,0:T(8,128)(2,1)}), bf16[1,256,256]{2,1,0:T(8,128)(2,1)}) %reduce-scatter.11.cloned.1.call-update) | async-done | bytes 131088 | tf_op jit(solution)/shard_map/reduce_scatter | solution.py:237
  310.4 23.0 %reduce-scatter.9.cloned.1.call-done = bf16[1,256,256]{2,1,0:T(8,128)(2,1)} async-done(((bf16[1,1024,256]{2,1,0:T(8,128)(2,1)}), bf16[1,256,256]{2,1,0:T(8,128)(2,1)}) %reduce-scatter.9.cloned.1.call-update) | async-done | bytes 131088 | tf_op jit(solution)/shard_map/reduce_scatter | solution.py:231
  333.4 2.9 fusion.50
  336.4 3.4 convolution_convert_fusion.1
  339.9 3.3 convolution_convert_fusion
  343.3 0.8 copy-done.26
  344.1 1.5 convolution_convert_fusion.2
  345.6 1.6 copy.63
  347.4 50.3 %reduce-scatter.13.cloned.1.call-done = bf16[128,256]{1,0:T(8,128)(2,1)} async-done(((bf16[1024,256]{1,0:T(8,128)(2,1)}), bf16[128,256]{1,0:T(8,128)(2,1)}) %reduce-scatter.13.cloned.1.call-update) | async-done | bytes 65552 | tf_op jit(solution)/shard_map/reduce_scatter | solution.py:267
  397.7 1.5 convert_element_type.243
  399.3 35.9 %all-reduce = (f32[2,256]{1,0:T(2,128)}, f32[1024]{0:T(1024)}, f32[2,1024]{1,0:T(2,128)}, f32[2,1024]{1,0:T(2,128)}, f32[2,1024]{1,0:T(2,128)}) all-reduce(f32[2,256]{1,0:T(2,128)S(1)} %pad_maximum_fusion.6, f32[1024]{0:T(1024)S(1)} %get-tuple-element.288, ...), channel_id=1, replica_groups=mesh['weight'=2,'ctx'=4,'tensor'=4] {'weight','ctx'}, use_global_device_ids=true, to_apply=%region_27.28 | all-reduce | flops 7680 | bytes 61440 | tf_op jit(solution)/shard_map/psum | solution.py:277
  435.2 2.0 add_convert_fusion
  437.2 68.2 %reduce-scatter.15.cloned.1.call-done = bf16[128,1024]{1,0:T(8,128)(2,1)} async-done(((bf16[1024,1024]{1,0:T(8,128)(2,1)}), bf16[128,1024]{1,0:T(8,128)(2,1)}) %reduce-scatter.15.cloned.1.call-update) | async-done | bytes 262160 | tf_op jit(solution)/shard_map/reduce_scatter | solution.py:270
  505.4 1.8 convert_element_type.245
  507.2 69.1 %reduce-scatter.17.cloned.1.call-done = bf16[128,1024]{1,0:T(8,128)(2,1)} async-done(((bf16[1024,1024]{1,0:T(8,128)(2,1)}), bf16[128,1024]{1,0:T(8,128)(2,1)}) %reduce-scatter.17.cloned.1.call-update) | async-done | bytes 262160 | tf_op jit(solution)/shard_map/reduce_scatter | solution.py:273
  576.3 1.8 convert_element_type.247
  578.1 66.3 %reduce-scatter.19.cloned.1.call-done = bf16[128,768]{1,0:T(8,128)(2,1)} async-done(((bf16[1024,768]{1,0:T(8,128)(2,1)}), bf16[128,768]{1,0:T(8,128)(2,1)}) %reduce-scatter.19.cloned.1.call-update) | async-done | bytes 196624
  644.3 1.1 copy.64
  645.4 0.9 copy.54
  (152 shorter events, 9.7 us)
Async XLA Ops:
  7.2 2.5 copy-start.30
  7.2 2.6 copy-start.25
  7.2 32.5 %copy-start.2 = (bf16[1,256,1024]{2,1,0:T(8,128)(2,1)S(1)}, bf16[1,256,1024]{2,1,0:T(8,128)(2,1)}, u32[]{:S(2)}) copy-start(bf16[1,256,1024]{2,1,0:T(8,128)(2,1)} %param.15) | copy-start | bytes 1572868
  7.2 32.5 %all-gather.5.cloned.1.call-start = ((), (), s32[]{:S(2)}) async-start(), calls=%async_computation.6 | async-start | bytes 2359296 | tf_op jit(solution)/shard_map/all_gather | solution.py:101
  9.6 108.6 %all-reduce.6.cloned.1.call-start = ((), (), s32[]{:S(2)}) async-start(), calls=%async_computation.7 | async-start | bytes 1048576 | tf_op jit(solution)/shard_map/psum | solution.py:44
  81.6 4.3 copy-start.12
  81.6 4.3 copy-start.27
  81.6 4.3 copy-start.28
  81.6 4.4 copy-start.29
  81.7 0.7 copy-start.21
  84.6 68.5 %copy-start.33 = (f32[1024]{0:T(1024)S(1)}, f32[1024]{0:T(1024)}, u32[]{:S(2)}) copy-start(f32[1024]{0:T(1024)} %param.21) | copy-start | bytes 12292
  84.6 68.5 %all-gather.7.cloned.1.call-start = ((), (), s32[]{:S(2)}) async-start(), calls=%async_computation.8 | async-start | bytes 3145728 | tf_op jit(solution)/shard_map/all_gather | solution.py:103
  85.3 102.3 %all-gather.9.cloned.1.call-start = ((), (), s32[]{:S(2)}) async-start(), calls=%async_computation.9 | async-start | bytes 3145728 | tf_op jit(solution)/shard_map/all_gather | solution.py:104
  85.9 138.4 %all-reduce.8.cloned.1.call-start = ((), (), s32[]{:S(2)}) async-start(), calls=%async_computation.10 | async-start | bytes 1048576 | tf_op jit(solution)/shard_map/psum | solution.py:44
  118.3 34.8 %copy-start.9 = (bf16[1,256,1024]{2,1,0:T(8,128)(2,1)S(1)}, bf16[1,256,1024]{2,1,0:T(8,128)(2,1)}, u32[]{:S(2)}) copy-start(bf16[1,256,1024]{2,1,0:T(8,128)(2,1)} %all-reduce.6.cloned.1.call-done) | copy-start | bytes 1572868
  155.5 35.2 %copy-start.23 = (f32[256,1024]{1,0:T(8,128)}, f32[256,1024]{1,0:T(8,128)S(1)}, u32[]{:S(2)}) copy-start(f32[256,1024]{1,0:T(8,128)S(1)} %convolution_add_fusion) | copy-start | bytes 3145732
  190.7 35.5 %copy-start.17 = (bf16[1,256,1024]{2,1,0:T(8,128)(2,1)S(1)}, bf16[1,256,1024]{2,1,0:T(8,128)(2,1)}, u32[]{:S(2)}) copy-start(bf16[1,256,1024]{2,1,0:T(8,128)(2,1)} %param.25) | copy-start | bytes 1572868
  190.7 74.6 %all-reduce.10.cloned.1.call-start = ((), (), s32[]{:S(2)}) async-start(), calls=%async_computation.11 | async-start | bytes 1048576 | tf_op jit(solution)/shard_map/psum | solution.py:44
  224.3 2.5 copy-start.18
  226.2 1.8 copy-start.24
  226.3 1.9 copy-start.32
  228.0 39.2 %copy-start.7 = (f32[1,256,1024]{2,1,0:T(8,128)}, f32[1,256,1024]{2,1,0:T(8,128)S(1)}, u32[]{:S(2)}) copy-start(f32[1,256,1024]{2,1,0:T(8,128)S(1)} %get-tuple-element.276) | copy-start | bytes 3145732
  228.2 1.9 copy-start.31
  229.2 38.0 %copy-start.34 = (bf16[256,1024]{1,0:T(8,128)(2,1)}, bf16[256,1024]{1,0:T(8,128)(2,1)S(1)}, u32[]{:S(2)}) copy-start(bf16[256,1024]{1,0:T(8,128)(2,1)S(1)} %get-tuple-element.289) | copy-start | bytes 1572868
  229.2 36.1 %copy-start.10 = (bf16[1,256,1024]{2,1,0:T(8,128)(2,1)S(1)}, bf16[1,256,1024]{2,1,0:T(8,128)(2,1)}, u32[]{:S(2)}) copy-start(bf16[1,256,1024]{2,1,0:T(8,128)(2,1)} %all-reduce.6.cloned.1.call-done) | copy-start | bytes 1572868
  231.7 78.7 %reduce-scatter.11.cloned.1.call-start = ((), (), s32[]{:S(2)}) async-start(), calls=%async_computation.13 | async-start | bytes 655360 | tf_op jit(solution)/shard_map/reduce_scatter | solution.py:237
  265.3 1.9 copy-start.16
  267.2 1.6 copy-start.15
  267.3 1.9 copy-start.13
  267.8 1.0 copy-start.5
  270.9 1.8 copy-start
  272.3 1.0 copy-start.4
  274.0 3.2 copy-start.19
  277.2 1.3 copy-start.1
  277.7 0.8 copy-start.20
  278.5 1.8 copy-start
  279.8 1.0 copy-start.4
  281.6 3.3 copy-start.19
  284.9 1.3 copy-start.1
  285.4 0.8 copy-start.20
  286.2 4.3 copy-start.6
  286.2 4.3 copy-start.22
  288.3 3.5 copy-start.14
  288.3 45.1 %reduce-scatter.9.cloned.1.call-start = ((), (), s32[]{:S(2)}) async-start(), calls=%async_computation.12 | async-start | bytes 655360 | tf_op jit(solution)/shard_map/reduce_scatter | solution.py:231
  290.4 107.3 %reduce-scatter.13.cloned.1.call-start = ((), (), s32[]{:S(2)}) async-start(), calls=%async_computation.15 | async-start | bytes 589824 | tf_op jit(solution)/shard_map/reduce_scatter | solution.py:267
  291.7 143.5 %all-reduce.12.cloned.1.call-start = ((), (), s32[]{:S(2)}) async-start(), calls=%async_computation.14 | async-start | bytes 1048576 | tf_op jit(solution)/shard_map/psum | solution.py:44
  291.8 44.6 %copy-start.3 = (bf16[1,256,1024]{2,1,0:T(8,128)(2,1)S(1)}, bf16[1,256,1024]{2,1,0:T(8,128)(2,1)}, u32[]{:S(2)}) copy-start(bf16[1,256,1024]{2,1,0:T(8,128)(2,1)} %param.15) | copy-start | bytes 1572868
  291.8 44.6 %copy-start.11 = (bf16[1,256,1024]{2,1,0:T(8,128)(2,1)S(1)}, bf16[1,256,1024]{2,1,0:T(8,128)(2,1)}, u32[]{:S(2)}) copy-start(bf16[1,256,1024]{2,1,0:T(8,128)(2,1)} %all-reduce.6.cloned.1.call-done) | copy-start | bytes 1572868
  336.3 3.5 copy-start.8
  336.3 169.1 %reduce-scatter.15.cloned.1.call-start = ((), (), s32[]{:S(2)}) async-start(), calls=%async_computation.16 | async-start | bytes 2359296 | tf_op jit(solution)/shard_map/reduce_scatter | solution.py:270
  339.8 236.5 %reduce-scatter.17.cloned.1.call-start = ((), (), s32[]{:S(2)}) async-start(), calls=%async_computation.17 | async-start | bytes 2359296 | tf_op jit(solution)/shard_map/reduce_scatter | solution.py:273
  343.2 0.9 copy-start.26
  343.2 301.1 %reduce-scatter.19.cloned.1.call-start = ((), (), s32[]{:S(2)}) async-start(), calls=%async_computation.18 | async-start | bytes 1769472
Sparse Core Ops, SparseCore 0:
  9.8 29.8 all-gather.4
  84.7 33.5 all-reduce.5
  119.8 33.1 all-gather.6
  154.4 33.0 all-gather.8
  190.8 33.4 all-reduce.7
  231.8 33.5 all-reduce.9
  288.4 21.8 reduce-scatter.10
  313.2 20.1 reduce-scatter.8
  336.7 60.9 reduce-scatter.12
  400.5 32.4 all-reduce.11
  436.5 68.8 reduce-scatter.14
  508.8 67.4 reduce-scatter.16
  579.7 64.6 reduce-scatter.18
where the time goes:
time: 654 us; the launch traced here: 653 us
  waiting for transfers between devices  480 us (73%)
  blocking collectives  78.3 us (12%)
  matrix products  38.7 us (6%)
  local copies, waits for them, and re-layouts  20.9 us (3%)
  other arithmetic  17.2 us (3%)
  between operations  14.5 us (2%)
    psum x4, waiting for transfers between devices, settle(): lax.psum(partial_value.astype(jnp.bfloat16), 'tensor').astype(jnp.float32)  99.2 us
    reduce_scatter x1, waiting for transfers between devices, local(): lax.psum_scatter(grad_down_w.astype(jnp.bfloat16), ('weight', 'ctx'), sca...  69.1 us
    reduce_scatter x1, waiting for transfers between devices, local(): lax.psum_scatter(grad_up_w.astype(jnp.bfloat16), ('weight', 'ctx'), scatt...  68.2 us
    unnamed x14, waiting for transfers between devices  67.7 us
    reduce_scatter x1, waiting for transfers between devices, local(): lax.psum_scatter(grad_out_w.astype(jnp.bfloat16), ('weight', 'ctx'), scat...  50.3 us
    psum x1, blocking collectives, local(): lax.psum((grad_heads_bias, grad_up_b, jnp.stack([bias_out, bias_down]), j...  35.9 us
    all_gather x1, waiting for transfers between devices, local(): lax.all_gather(w_down, 'weight', axis=0, tiled=True)  32.1 us
    all_gather x1, waiting for transfers between devices, local(): lax.all_gather(w_up, 'weight', axis=0, tiled=True)  32 us
  transfers between devices with their start and end apart: 13, of which 12 were waited for; matrix products, arithmetic and copies ran while one was open for 4% of the time, Pallas kernels for 0%

commit v1 on v0

--- a/solution.py
+++ b/solution.py
@@ -275,14 +275,17 @@
         ).astype(jnp.float32),
     )
     vector_sums = lax.psum(
-        (
-            grad_heads_bias,
-            grad_up_b,
-            jnp.stack([bias_out, bias_down]),
-            jnp.stack([gain_one, gain_two]),
-            jnp.stack([shift_one, shift_two]),
+        lax.psum(
+            (
+                grad_heads_bias,
+                grad_up_b,
+                jnp.stack([bias_out, bias_down]),
+                jnp.stack([gain_one, gain_two]),
+                jnp.stack([shift_one, shift_two]),
+            ),
+            "weight",
         ),
-        ("weight", "ctx"),
+        "ctx",
     )
     return (
         layer_out,

time: 654 us -> 654 us (level)
  blocking collectives: 78.3 us -> 68.2 us
  waiting for transfers between devices: 480 us -> 490 us
    psum x1, blocking collectives: 35.9 us -> 8.16 us  [local(): lax.psum((grad_heads_bias, grad_up_b, jnp.stack([bias_out, bias_down]), j...]
    psum x0 -> x1, blocking collectives: none -> 17.8 us  [local(): lax.psum(lax.psum((grad_heads_bias, grad_up_b, jnp.stack([bias_out, bias_...]
    psum x4, waiting for transfers between devices: 99.2 us -> 107 us  [settle(): lax.psum(partial_value.astype(jnp.bfloat16), 'tensor').astype(jnp.float32)]
  transfers between devices with their start and end apart: 13 -> 13, of which waited for: 12 -> 13; matrix products, arithmetic and copies ran while one was open for 4% -> 4% of each run, Pallas kernels for 0% -> 0%
where the time goes in v1:
time: 654 us; the launch traced here: 653 us
  waiting for transfers between devices  490 us (75%)
  blocking collectives  68.2 us (10%)
  matrix products  38.7 us (6%)
  local copies, waits for them, and re-layouts  20.9 us (3%)
  other arithmetic  17.2 us (3%)
  between operations  14.5 us (2%)
    psum x4, waiting for transfers between devices, settle(): lax.psum(partial_value.astype(jnp.bfloat16), 'tensor').astype(jnp.float32)  107 us
    reduce_scatter x1, waiting for transfers between devices, local(): lax.psum_scatter(grad_up_w.astype(jnp.bfloat16), ('weight', 'ctx'), scatt...  70.5 us
    reduce_scatter x1, waiting for transfers between devices, local(): lax.psum_scatter(grad_down_w.astype(jnp.bfloat16), ('weight', 'ctx'), sca...  69.1 us
    unnamed x14, waiting for transfers between devices  67.8 us
    reduce_scatter x1, waiting for transfers between devices, local(): lax.psum_scatter(grad_out_w.astype(jnp.bfloat16), ('weight', 'ctx'), scat...  50.3 us
    all_gather x1, waiting for transfers between devices, local(): lax.all_gather(w_down, 'weight', axis=0, tiled=True)  32.1 us
    all_gather x1, waiting for transfers between devices, local(): lax.all_gather(w_up, 'weight', axis=0, tiled=True)  32 us
    reduce_scatter x1, waiting for transfers between devices, local(): lax.psum_scatter(grad_keys_all.reshape(batch, key_rows, head_cols).astype...  23 us
  transfers between devices with their start and end apart: 13, of which 13 were waited for; matrix products, arithmetic and copies ran while one was open for 4% of the time, Pallas kernels for 0%

profile of v1, /device:TPU:0, one launch (start us, length us, event | category | flops | bytes accessed | tf_op | source)
XLA Modules:
  0.0 653.0 jit_solution(13501467801954487957)
XLA Ops:
  7.3 2.4 copy.48
  9.8 10.0 %all_gather.23 = bf16[1024,256]{1,0:T(8,128)(2,1)} all-gather(bf16[512,256]{1,0:T(8,128)(2,1)S(1)} %copy-done.25), channel_id=1, replica_groups=mesh['weight'=2,'ctx'=4,'tensor'=4] {'weight'}, dimensions={0}, use_global_device_ids=true | all-gather | bytes 786432 | tf_op jit(solution)/shard_map/all_gather | solution.py:102
  19.8 19.8 %all-gather.5.cloned.1.call-done = bf16[1024,3,256]{0,2,1:T(8,128)(2,1)} async-done(((bf16[512,3,256]{0,2,1:T(8,128)(2,1)}), bf16[1024,3,256]{0,2,1:T(8,128)(2,1)}) %all-gather.5.cloned.1.call-update) | async-done | bytes 1572880 | tf_op jit(solution)/shard_map/all_gather | solution.py:101
  39.7 2.0 convolution_bitcast_fusion.5
  41.8 15.5 %all-gather = bf16[1,1024,1,256]{1,3,2,0:T(8,128)(2,1)S(1)} all-gather(bf16[1,256,1,256]{1,3,2,0:T(8,128)(2,1)S(1)} %slice.57), channel_id=2, replica_groups=mesh['weight'=2,'ctx'=4,'tensor'=4] {'ctx'}, dimensions={1}, use_global_device_ids=true | all-gather | bytes 655360 | tf_op jit(solution)/shard_map/all_gather | solution.py:119
  57.3 16.8 %all_gather.22 = bf16[1,1024,256]{1,2,0:T(8,128)(2,1)} all-gather(bf16[1,256,256]{1,2,0:T(8,128)(2,1)S(1)} %fusion.72), channel_id=1, replica_groups=mesh['weight'=2,'ctx'=4,'tensor'=4] {'ctx'}, dimensions={1}, use_global_device_ids=true | all-gather | bytes 655360 | tf_op jit(solution)/shard_map/all_gather | solution.py:120
  74.3 7.3 %while.30 = (s32[]{:T(128)}, f32[1,256,4,64]{1,3,2,0:T(8,128)S(1)}, f32[1,256,4]{1,2,0:T(4,128)S(1)}, f32[1,256,4]{1,2,0:T(4,128)S(1)}, s32[2]{0:T(128)S(1)}, /*...) while((s32[]{:T(128)}, f32[1,256,4,64]{1,3,2,0:T(8,128)S(1)}, ...), condition=%wide.region_3.4_spmd.clone, body=%wide.region_0.3_spmd.clone.sunk | while | flops 138614784 | bytes 7536843 | solution.py:79
  76.1 1.5 fusion.129
  79.7 1.5 fusion.129
  82.3 2.2 fusion.53
  84.6 0.7 all-gather.7.cloned.1.call-update
  86.0 32.2 %all-reduce.7.cloned.1.call-done = bf16[1,256,1024]{2,1,0:T(8,128)(2,1)} async-done(((bf16[1,256,1024]{2,1,0:T(8,128)(2,1)}), bf16[1,256,1024]{2,1,0:T(8,128)(2,1)}) %all-reduce.7.cloned.1.call-update) | async-done | bytes 524304 | tf_op jit(solution)/shard_map/psum | solution.py:44
  118.3 1.4 fusion.63
  119.6 1.4 multiply_reduce_fusion.3
  121.0 32.0 %all-gather.7.cloned.1.call-done = bf16[1024,1024]{1,0:T(8,128)(2,1)} async-done(((bf16[512,1024]{1,0:T(8,128)(2,1)}), bf16[1024,1024]{1,0:T(8,128)(2,1)}) %all-gather.7.cloned.1.call-update) | async-done | bytes 2097168 | tf_op jit(solution)/shard_map/all_gather | solution.py:103
  153.0 2.4 convolution_add_fusion
  155.5 32.1 %all-gather.9.cloned.1.call-done = bf16[1024,1024]{1,0:T(8,128)(2,1)} async-done(((bf16[512,1024]{1,0:T(8,128)(2,1)}), bf16[1024,1024]{1,0:T(8,128)(2,1)}) %all-gather.9.cloned.1.call-update) | async-done | bytes 2097168 | tf_op jit(solution)/shard_map/all_gather | solution.py:104
  187.6 3.1 fusion.51
  190.8 33.5 %all-reduce.9.cloned.1.call-done = bf16[1,256,1024]{2,1,0:T(8,128)(2,1)} async-done(((bf16[1,256,1024]{2,1,0:T(8,128)(2,1)}), bf16[1,256,1024]{2,1,0:T(8,128)(2,1)}) %all-reduce.9.cloned.1.call-update) | async-done | bytes 524304 | tf_op jit(solution)/shard_map/psum | solution.py:44
  224.3 1.7 fusion.85
  226.8 1.2 fusion.55
  228.2 1.0 fusion.91
  229.2 0.8 copy-done.31
  230.0 1.6 fusion.52
  231.9 33.4 %all-reduce.11.cloned.1.call-done = bf16[1,256,1024]{2,1,0:T(8,128)(2,1)} async-done(((bf16[1,256,1024]{2,1,0:T(8,128)(2,1)}), bf16[1,256,1024]{2,1,0:T(8,128)(2,1)}) %all-reduce.11.cloned.1.call-update) | async-done | bytes 524304 | tf_op jit(solution)/shard_map/psum | solution.py:44
  265.3 1.9 multiply_reduce_fusion
  267.8 1.0 copy-done.5
  269.2 0.9 broadcast_in_dim.10
  270.1 0.9 broadcast_in_dim.10.clone
  270.9 15.2 %while.31 = (s32[]{:T(128)}, f32[1,256,4,64]{1,3,2,0:T(8,128)}, bf16[1,1024,4,64]{1,3,2,0:T(8,128)(2,1)}, bf16[1,1024,4,64]{1,3,2,0:T(8,128)(2,1)}, s32[2]{0:T(1...) while((s32[]{:T(128)}, f32[1,256,4,64]{1,3,2,0:T(8,128)}, ...), condition=%wide.region_17.18_spmd.clone, body=%wide.region_16.17_spmd.clone.sunk | while | flops 340393984 | bytes 22819192 | solution.py:228
  270.9 0.7 dynamic_slice.60
  273.3 0.7 fusion.142
  274.1 2.0 fusion.143
  276.1 1.1 fusion.144
  277.7 0.8 copy-done.20
  278.5 0.7 dynamic_slice.60
  280.9 0.7 fusion.142
  281.6 2.1 fusion.143
  283.7 1.1 fusion.144
  285.4 0.8 copy-done.20
  286.2 2.1 copy.50
  288.4 2.0 copy.49
  290.5 1.2 convolution_convert_fusion.3
  292.0 18.3 %reduce-scatter.11.cloned.1.call-done = bf16[1,256,256]{2,1,0:T(8,128)(2,1)} async-done(((bf16[1,1024,256]{2,1,0:T(8,128)(2,1)}), bf16[1,256,256]{2,1,0:T(8,128)(2,1)}) %reduce-scatter.11.cloned.1.call-update) | async-done | bytes 131088 | tf_op jit(solution)/shard_map/reduce_scatter | solution.py:237
  310.4 23.0 %reduce-scatter.9.cloned.1.call-done = bf16[1,256,256]{2,1,0:T(8,128)(2,1)} async-done(((bf16[1,1024,256]{2,1,0:T(8,128)(2,1)}), bf16[1,256,256]{2,1,0:T(8,128)(2,1)}) %reduce-scatter.9.cloned.1.call-update) | async-done | bytes 131088 | tf_op jit(solution)/shard_map/reduce_scatter | solution.py:231
  333.4 2.9 fusion.50
  336.4 3.4 convolution_convert_fusion.1
  339.9 3.3 convolution_convert_fusion
  343.3 0.8 copy-done.26
  344.1 1.5 convolution_convert_fusion.2
  345.6 1.6 copy.63
  347.4 50.3 %reduce-scatter.13.cloned.1.call-done = bf16[128,256]{1,0:T(8,128)(2,1)} async-done(((bf16[1024,256]{1,0:T(8,128)(2,1)}), bf16[128,256]{1,0:T(8,128)(2,1)}) %reduce-scatter.13.cloned.1.call-update) | async-done | bytes 65552 | tf_op jit(solution)/shard_map/reduce_scatter | solution.py:267
  397.7 1.5 convert_element_type.243
  399.3 8.2 %all-reduce.1 = (f32[2,256]{1,0:T(2,128)S(1)}, f32[1024]{0:T(1024)S(1)}, f32[2,1024]{1,0:T(2,128)S(1)}, f32[2,1024]{1,0:T(2,128)S(1)}, f32[2,1024]{1,0:T(2,128)S(1)}) all-reduce(f32[2,256]{1,0:T(2,128)S(1)} %pad_maximum_fusion.6, f32[1024]{0:T(1024)S(1)} %get-tuple-element.293, ...), channel_id=1, replica_groups=mesh['weight'=2,'ctx'=4,'tensor'=4] {'weight'}, use_global_device_ids=true, to_apply=%region_27.28 | all-reduce | flops 7680 | bytes 61440 | tf_op jit(solution)/shard_map/psum | solution.py:278
  407.4 17.8 %all-reduce = (f32[2,256]{1,0:T(2,128)}, f32[1024]{0:T(1024)}, f32[2,1024]{1,0:T(2,128)}, f32[2,1024]{1,0:T(2,128)}, f32[2,1024]{1,0:T(2,128)}) all-reduce(f32[2,256]{1,0:T(2,128)S(1)} %get-tuple-element.268, f32[1024]{0:T(1024)S(1)} %get-tuple-element.269, ...), channel_id=1, replica_groups=mesh['weight'=2,'ctx'=4,'tensor'=4] {'ctx'}, use_global_device_ids=true, to_apply=%region_28.29 | all-reduce | flops 7680 | bytes 61440 | tf_op jit(solution)/shard_map/psum | solution.py:277
  425.2 7.7 %all-reduce.13.cloned.1.call-done = bf16[1,256,1024]{2,1,0:T(8,128)(2,1)} async-done(((bf16[1,256,1024]{2,1,0:T(8,128)(2,1)}), bf16[1,256,1024]{2,1,0:T(8,128)(2,1)}) %all-reduce.13.cloned.1.call-update) | async-done | bytes 524304 | tf_op jit(solution)/shard_map/psum | solution.py:44
  433.0 2.0 add_convert_fusion
  434.9 70.5 %reduce-scatter.15.cloned.1.call-done = bf16[128,1024]{1,0:T(8,128)(2,1)} async-done(((bf16[1024,1024]{1,0:T(8,128)(2,1)}), bf16[128,1024]{1,0:T(8,128)(2,1)}) %reduce-scatter.15.cloned.1.call-update) | async-done | bytes 262160 | tf_op jit(solution)/shard_map/reduce_scatter | solution.py:270
  505.4 1.8 convert_element_type.245
  507.2 69.1 %reduce-scatter.17.cloned.1.call-done = bf16[128,1024]{1,0:T(8,128)(2,1)} async-done(((bf16[1024,1024]{1,0:T(8,128)(2,1)}), bf16[128,1024]{1,0:T(8,128)(2,1)}) %reduce-scatter.17.cloned.1.call-update) | async-done | bytes 262160 | tf_op jit(solution)/shard_map/reduce_scatter | solution.py:273
  576.3 1.8 convert_element_type.247
  578.1 66.4 %reduce-scatter.19.cloned.1.call-done = bf16[128,768]{1,0:T(8,128)(2,1)} async-done(((bf16[1024,768]{1,0:T(8,128)(2,1)}), bf16[128,768]{1,0:T(8,128)(2,1)}) %reduce-scatter.19.cloned.1.call-update) | async-done | bytes 196624
  644.5 1.1 copy.64
  645.6 0.9 copy.54
  (153 shorter events, 10.9 us)
Async XLA Ops:
  7.2 2.5 copy-start.30
  7.2 2.6 copy-start.25
  7.2 32.5 %copy-start.2 = (bf16[1,256,1024]{2,1,0:T(8,128)(2,1)S(1)}, bf16[1,256,1024]{2,1,0:T(8,128)(2,1)}, u32[]{:S(2)}) copy-start(bf16[1,256,1024]{2,1,0:T(8,128)(2,1)} %param.15) | copy-start | bytes 1572868
  7.2 32.5 %all-gather.5.cloned.1.call-start = ((), (), s32[]{:S(2)}) async-start(), calls=%async_computation.6 | async-start | bytes 2359296 | tf_op jit(solution)/shard_map/all_gather | solution.py:101
  9.6 108.6 %all-reduce.7.cloned.1.call-start = ((), (), s32[]{:S(2)}) async-start(), calls=%async_computation.7 | async-start | bytes 1048576 | tf_op jit(solution)/shard_map/psum | solution.py:44
  81.6 4.3 copy-start.12
  81.6 4.3 copy-start.27
  81.6 4.3 copy-start.28
  81.6 4.4 copy-start.29
  81.7 0.7 copy-start.21
  84.6 68.5 %copy-start.33 = (f32[1024]{0:T(1024)S(1)}, f32[1024]{0:T(1024)}, u32[]{:S(2)}) copy-start(f32[1024]{0:T(1024)} %param.21) | copy-start | bytes 12292
  84.6 68.5 %all-gather.7.cloned.1.call-start = ((), (), s32[]{:S(2)}) async-start(), calls=%async_computation.8 | async-start | bytes 3145728 | tf_op jit(solution)/shard_map/all_gather | solution.py:103
  85.3 102.3 %all-gather.9.cloned.1.call-start = ((), (), s32[]{:S(2)}) async-start(), calls=%async_computation.9 | async-start | bytes 3145728 | tf_op jit(solution)/shard_map/all_gather | solution.py:104
  85.9 138.4 %all-reduce.9.cloned.1.call-start = ((), (), s32[]{:S(2)}) async-start(), calls=%async_computation.10 | async-start | bytes 1048576 | tf_op jit(solution)/shard_map/psum | solution.py:44
  118.3 34.8 %copy-start.9 = (bf16[1,256,1024]{2,1,0:T(8,128)(2,1)S(1)}, bf16[1,256,1024]{2,1,0:T(8,128)(2,1)}, u32[]{:S(2)}) copy-start(bf16[1,256,1024]{2,1,0:T(8,128)(2,1)} %all-reduce.7.cloned.1.call-done) | copy-start | bytes 1572868
  155.5 35.2 %copy-start.23 = (f32[256,1024]{1,0:T(8,128)}, f32[256,1024]{1,0:T(8,128)S(1)}, u32[]{:S(2)}) copy-start(f32[256,1024]{1,0:T(8,128)S(1)} %convolution_add_fusion) | copy-start | bytes 3145732
  190.7 35.5 %copy-start.17 = (bf16[1,256,1024]{2,1,0:T(8,128)(2,1)S(1)}, bf16[1,256,1024]{2,1,0:T(8,128)(2,1)}, u32[]{:S(2)}) copy-start(bf16[1,256,1024]{2,1,0:T(8,128)(2,1)} %param.25) | copy-start | bytes 1572868
  190.7 74.6 %all-reduce.11.cloned.1.call-start = ((), (), s32[]{:S(2)}) async-start(), calls=%async_computation.11 | async-start | bytes 1048576 | tf_op jit(solution)/shard_map/psum | solution.py:44
  224.3 2.5 copy-start.18
  226.2 1.8 copy-start.24
  226.3 1.9 copy-start.32
  228.0 39.2 %copy-start.7 = (f32[1,256,1024]{2,1,0:T(8,128)}, f32[1,256,1024]{2,1,0:T(8,128)S(1)}, u32[]{:S(2)}) copy-start(f32[1,256,1024]{2,1,0:T(8,128)S(1)} %get-tuple-element.281) | copy-start | bytes 3145732
  228.2 1.9 copy-start.31
  229.2 38.0 %copy-start.34 = (bf16[256,1024]{1,0:T(8,128)(2,1)}, bf16[256,1024]{1,0:T(8,128)(2,1)S(1)}, u32[]{:S(2)}) copy-start(bf16[256,1024]{1,0:T(8,128)(2,1)S(1)} %get-tuple-element.294) | copy-start | bytes 1572868
  229.2 36.1 %copy-start.10 = (bf16[1,256,1024]{2,1,0:T(8,128)(2,1)S(1)}, bf16[1,256,1024]{2,1,0:T(8,128)(2,1)}, u32[]{:S(2)}) copy-start(bf16[1,256,1024]{2,1,0:T(8,128)(2,1)} %all-reduce.7.cloned.1.call-done) | copy-start | bytes 1572868
  231.7 78.7 %reduce-scatter.11.cloned.1.call-start = ((), (), s32[]{:S(2)}) async-start(), calls=%async_computation.13 | async-start | bytes 655360 | tf_op jit(solution)/shard_map/reduce_scatter | solution.py:237
  265.3 1.9 copy-start.16
  267.2 1.6 copy-start.15
  267.3 1.9 copy-start.13
  267.8 1.0 copy-start.5
  270.9 1.8 copy-start
  272.3 1.0 copy-start.4
  274.0 3.2 copy-start.19
  277.2 1.3 copy-start.1
  277.7 0.8 copy-start.20
  278.5 1.8 copy-start
  279.8 1.0 copy-start.4
  281.6 3.3 copy-start.19
  284.9 1.3 copy-start.1
  285.4 0.8 copy-start.20
  286.2 4.3 copy-start.6
  286.2 4.3 copy-start.22
  288.3 3.5 copy-start.14
  288.3 45.1 %reduce-scatter.9.cloned.1.call-start = ((), (), s32[]{:S(2)}) async-start(), calls=%async_computation.12 | async-start | bytes 655360 | tf_op jit(solution)/shard_map/reduce_scatter | solution.py:231
  290.4 107.3 %reduce-scatter.13.cloned.1.call-start = ((), (), s32[]{:S(2)}) async-start(), calls=%async_computation.15 | async-start | bytes 589824 | tf_op jit(solution)/shard_map/reduce_scatter | solution.py:267
  291.7 141.2 %all-reduce.13.cloned.1.call-start = ((), (), s32[]{:S(2)}) async-start(), calls=%async_computation.14 | async-start | bytes 1048576 | tf_op jit(solution)/shard_map/psum | solution.py:44
  291.8 44.6 %copy-start.3 = (bf16[1,256,1024]{2,1,0:T(8,128)(2,1)S(1)}, bf16[1,256,1024]{2,1,0:T(8,128)(2,1)}, u32[]{:S(2)}) copy-start(bf16[1,256,1024]{2,1,0:T(8,128)(2,1)} %param.15) | copy-start | bytes 1572868
  291.8 44.6 %copy-start.11 = (bf16[1,256,1024]{2,1,0:T(8,128)(2,1)S(1)}, bf16[1,256,1024]{2,1,0:T(8,128)(2,1)}, u32[]{:S(2)}) copy-start(bf16[1,256,1024]{2,1,0:T(8,128)(2,1)} %all-reduce.7.cloned.1.call-done) | copy-start | bytes 1572868
  336.3 3.5 copy-start.8
  336.3 169.1 %reduce-scatter.15.cloned.1.call-start = ((), (), s32[]{:S(2)}) async-start(), calls=%async_computation.16 | async-start | bytes 2359296 | tf_op jit(solution)/shard_map/reduce_scatter | solution.py:270
  339.8 236.5 %reduce-scatter.17.cloned.1.call-start = ((), (), s32[]{:S(2)}) async-start(), calls=%async_computation.17 | async-start | bytes 2359296 | tf_op jit(solution)/shard_map/reduce_scatter | solution.py:273
  343.2 0.9 copy-start.26
  343.2 301.3 %reduce-scatter.19.cloned.1.call-start = ((), (), s32[]{:S(2)}) async-start(), calls=%async_computation.18 | async-start | bytes 1769472
Sparse Core Ops, SparseCore 0:
  9.8 29.8 all-gather.4
  84.7 33.5 all-reduce.6
  119.8 33.1 all-gather.6
  154.4 33.0 all-gather.8
  190.8 33.4 all-reduce.8
  231.8 33.5 all-reduce.10
  288.4 21.8 reduce-scatter.10
  313.2 20.1 reduce-scatter.8
  336.7 60.9 reduce-scatter.12
  400.5 32.4 all-reduce.12
  436.5 68.8 reduce-scatter.14
  508.8 67.4 reduce-scatter.16
  579.7 64.7 reduce-scatter.18
